TPU v7x, 256 devices: a whole 4x4x8 slice. The times are simulated.
256 devices in a mesh: wide: 32 (over x, y, core), narrow: 8 (over z).
Axes of the slice: x: 4, y: 4, z: 8, core: 2. Of those that a mesh axis runs over, the one named last changes fastest.
Arguments:
- sources: float32 [32, 8, 16, 2, 512], P('wide', 'narrow'), may hold values from -6 to 6
- schur_blocks: bfloat16 [32, 8, 2048, 2048], P('wide', 'narrow'), as said below
- scaling: float32 [32, 8, 2, 512], P('wide', 'narrow'), may hold values from 0.08 to 0.4
- coarse_basis: float32 [32, 8, 2, 2, 8, 512], P('wide', 'narrow'), may hold values from -0.09375 to 0.09375
- coarse_inverse: float32 [32, 80, 80], P('wide'), as said below
- face_sizes: int32 [32, 8, 2], P('wide', 'narrow'), may hold values from 0 to 512, as said below
- face_match: int32 [32, 8, 2, 512], P('wide', 'narrow'), may hold values from 0 to 511, as said below
- face_slots: int32 [32, 8, 4], P('wide', 'narrow'), may hold values from 0 to 3, each once within a row
- corner_slots: int32 [33, 9], replicated, may hold values from 0 to 319, as said below
Outputs:
- solution: float32 [32, 8, 16, 2, 512], P('wide', 'narrow')
- residual: float32 [32, 8, 16, 2, 512], P('wide', 'narrow')
Inputs may be any that keep to these rules, and one draw needn't show every extreme that they name: `face_sizes`: the east faces of the last wide index and the north faces of the last narrow index have 0 unknowns; every other face has 128 to 512, and some face has exactly 512. `face_match`: each block is a permutation of 0 to 511 that maps the positions below the size of the matching owned face onto themselves. `corner_slots`: distinct slots for distinct vertices; slot 319 is used. `schur_blocks`: each block is symmetric and positive definite. `coarse_inverse`: each block is symmetric and positive definite.
All inputs are finite; a program needn't handle non-finite values.
Results may differ from a plain program's by a relative error of at most 0.0052.
Values may be sent and summed in bfloat16 or wider, within the bound.
A program may use at most 64 MiB of HBM per device.

v0:
```python
import jax
import jax.numpy as jnp
from jax import lax
from jax.sharding import PartitionSpec as P

ITERS = 2
highest = lax.Precision.HIGHEST


def shifted(block, axis, distance):
    devices = range(lax.axis_size(axis))
    route = [(i - distance, i) for i in devices if i - distance in devices]
    return lax.ppermute(block, axis, route)


def body(
    sources,
    schur_blocks,
    scaling,
    coarse_basis,
    coarse_inverse,
    face_sizes,
    face_match,
    face_slots,
    corner_slots,
):
    wide_count = lax.axis_size("wide")
    wide_at = lax.axis_index("wide")
    narrow_at = lax.axis_index("narrow")
    nrhs_count = sources.shape[2]
    face_width = sources.shape[4]
    basis_count = coarse_basis.shape[4]
    block_order = coarse_inverse.shape[1]
    capacity = block_order // basis_count
    slot_count = capacity * wide_count
    places = lax.broadcasted_iota(jnp.int32, (2, face_width), 1)
    live_mask = (places < face_sizes[0, 0][:, None]).astype(jnp.float32)
    weights = scaling[0, 0] * live_mask
    vectors = coarse_basis[0, 0] * live_mask[:, None, None, :]
    forward = face_match[0, 0]
    source_rows = lax.broadcasted_iota(jnp.int32, (2, face_width, face_width), 1)
    match_table = (forward[:, None, :] == source_rows).astype(jnp.float32)
    match_narrow = match_table.astype(jnp.bfloat16)
    slot_table = (face_slots[0, 0][:, None] == jnp.arange(4, dtype=jnp.int32)[None, :]).astype(
        jnp.float32
    )
    matrix = schur_blocks[0, 0]
    square = lax.dynamic_slice(corner_slots, (wide_at, narrow_at), (2, 2))
    corner_ids = jnp.stack([square[1, 0], square[1, 1], square[0, 1], square[1, 1]])
    incidence = (corner_ids[:, None] == jnp.arange(slot_count, dtype=jnp.int32)[None, :]).astype(
        jnp.float32
    )
    inverse_block = coarse_inverse[0]
    initial = sources[0, 0] * live_mask[None]

    def finish(residual, solved_slots):
        local_values = jnp.dot(
            incidence, solved_slots, precision=highest, preferred_element_type=jnp.float32
        )
        local_values = local_values.reshape(2, 2, basis_count, nrhs_count)
        return weights[None] * residual + jnp.einsum(
            "femk,femr->rfk", vectors, local_values, precision=highest
        )

    def precondition(residual):
        partial_value = jnp.einsum("femk,rfk->femr", vectors, residual, precision=highest).reshape(
            4, basis_count * nrhs_count
        )
        dense_part = jnp.dot(
            incidence.T, partial_value, precision=highest, preferred_element_type=jnp.float32
        )
        owned_rows = lax.psum_scatter(dense_part, "wide", scatter_dimension=0, tiled=True)
        owner_block = lax.psum(owned_rows, "narrow").reshape(block_order, nrhs_count)
        solved = jnp.dot(
            inverse_block, owner_block, precision=highest, preferred_element_type=jnp.float32
        )
        all_solved = lax.all_gather(
            solved.reshape(capacity, basis_count * nrhs_count), "wide", axis=0, tiled=True
        )
        precond = finish(residual, all_solved)
        inner_value = lax.psum(jnp.sum(residual * precond, axis=(1, 2)), ("wide", "narrow"))
        return (precond, inner_value)

    residual = initial
    solution = jnp.zeros_like(initial)
    precond, inner_now = precondition(residual)
    direction = precond
    for iteration in range(ITERS):
        rounded = direction.astype(jnp.bfloat16)
        from_west = shifted(rounded[:, 0], "wide", 1)
        from_south = shifted(rounded[:, 1], "narrow", 1)
        west_face = jnp.dot(from_west, match_narrow[0], preferred_element_type=jnp.float32)
        south_face = jnp.dot(from_south, match_narrow[1], preferred_element_type=jnp.float32)
        stacked = jnp.stack(
            [
                rounded[:, 0].astype(jnp.float32),
                rounded[:, 1].astype(jnp.float32),
                west_face,
                south_face,
            ],
            axis=1,
        )
        slotted = jnp.einsum("rdk,ds->rsk", stacked, slot_table, precision=highest).astype(
            jnp.bfloat16
        )
        product = jnp.dot(
            slotted.reshape(nrhs_count, 4 * face_width), matrix, preferred_element_type=jnp.float32
        )
        by_face = jnp.einsum(
            "rsk,ds->rdk", product.reshape(nrhs_count, 4, face_width), slot_table, precision=highest
        )
        to_west = jnp.einsum("rk,mk->rm", by_face[:, 2], match_table[0], precision=highest)
        to_south = jnp.einsum("rk,mk->rm", by_face[:, 3], match_table[1], precision=highest)
        from_east = shifted(to_west, "wide", -1)
        from_north = shifted(to_south, "narrow", -1)
        summed_all = jnp.stack([by_face[:, 0] + from_east, by_face[:, 1] + from_north], axis=1)
        applied = summed_all * live_mask[None]
        curvature = lax.psum(jnp.sum(direction * applied, axis=(1, 2)), ("wide", "narrow"))
        step_size = inner_now / curvature
        solution = solution + step_size[:, None, None] * direction
        residual = residual - step_size[:, None, None] * applied
        if iteration + 1 < ITERS:
            precond, inner_new = precondition(residual)
            direction = precond + (inner_new / inner_now)[:, None, None] * direction
            inner_now = inner_new
    return (solution[None, None], residual[None, None])


def solution(mesh):
    placed = (
        P("wide", "narrow", None, None, None),
        P("wide", "narrow", None, None),
        P("wide", "narrow", None, None),
        P("wide", "narrow", None, None, None, None),
        P("wide", None, None),
        P("wide", "narrow", None),
        P("wide", "narrow", None, None),
        P("wide", "narrow", None),
        P(),
    )
    return jax.shard_map(
        body,
        mesh=mesh,
        in_specs=placed,
        out_specs=(P("wide", "narrow", None, None, None), P("wide", "narrow", None, None, None)),
        check_vma=False,
    )
```

profile of v0, /device:TPU:1, one launch (start us, length us, event | category | flops | bytes accessed | tf_op | source)
XLA Modules:
  0.0 640.1 jit_solution(5082868968421109135)
XLA Ops:
  10.6 2.1 pad_add_fusion
  16.4 110.0 %all-reduce.6.cloned.1.call-done = f32[320,128]{1,0:T(8,128)} async-done(((f32[320,128]{1,0:T(8,128)}), f32[320,128]{1,0:T(8,128)}) %all-reduce.6.cloned.1.call-update) | async-done | bytes 163856
  127.2 23.5 %psum.42 = f32[80,16]{1,0:T(8,128)S(1)} all-reduce(f32[80,16]{1,0:T(8,128)S(1)} %reshape.170), channel_id=1, replica_groups=mesh['wide'=32,'narrow'=8] {'narrow'}, use_global_device_ids=true, to_apply=%region_1.0 | all-reduce | flops 1280 | bytes 10240 | tf_op jit(solution)/shard_map/psum | solution.py:73
  151.1 30.1 %all-gather = f32[32,10,128]{2,1,0:T(8,128)S(1)} all-gather(f32[1,10,128]{2,1,0:T(8,128)S(1)} %reshape.179), channel_id=1, replica_groups=mesh['wide'=32,'narrow'=8] {'wide'}, dimensions={0}, use_global_device_ids=true | all-gather | bytes 168960 | tf_op jit(solution)/shard_map/all_gather | solution.py:77
  182.7 1.3 collective-permute-start.1
  185.3 12.3 %copy.57 = bf16[2048,2048]{1,0:T(8,128)(2,1)} copy(bf16[2048,2048]{0,1:T(8,128)(2,1)} %bitcast.206) | data formatting | bytes 16777216 | tf_op jit(solution)/shard_map/dot_general | solution.py:106
  197.6 2.6 collective-permute-start
  201.7 5.6 fusion.60
  208.9 1.3 collective-permute-start.3
  210.2 1.9 collective-permute-start.2
  212.1 2.1 collective-permute-done.3
  214.2 1.7 collective-permute-done.2
  216.1 78.5 %all-reduce.2 = (f32[16]{0:T(128)S(1)}, f32[16]{0:T(128)S(1)}) all-reduce(f32[16]{0:T(128)S(1)} %get-tuple-element.9, f32[16]{0:T(128)S(1)} %get-tuple-element.8), channel_id=1, replica_groups=mesh['wide'=32,'narrow'=8] {'wide','narrow'}, use_global_device_ids=true, to_apply=%region_3.0 | all-reduce | flops 32 | bytes 256 | tf_op jit(solution)/shard_map/psum | solution.py:81
  296.1 106.8 %all-reduce.8.cloned.1.call-done = f32[320,128]{1,0:T(8,128)} async-done(((f32[320,128]{1,0:T(8,128)}), f32[320,128]{1,0:T(8,128)}) %all-reduce.8.cloned.1.call-update) | async-done | bytes 163856
  403.7 23.5 %psum.45 = f32[80,16]{1,0:T(8,128)S(1)} all-reduce(f32[80,16]{1,0:T(8,128)S(1)} %reshape.175), channel_id=1, replica_groups=mesh['wide'=32,'narrow'=8] {'narrow'}, use_global_device_ids=true, to_apply=%region_7.0 | all-reduce | flops 1280 | bytes 10240 | tf_op jit(solution)/shard_map/psum | solution.py:73
  427.6 30.1 %all-gather.1 = f32[32,10,128]{2,1,0:T(8,128)S(1)} all-gather(f32[1,10,128]{2,1,0:T(8,128)S(1)} %reshape.181), channel_id=1, replica_groups=mesh['wide'=32,'narrow'=8] {'wide'}, dimensions={0}, use_global_device_ids=true | all-gather | bytes 168960 | tf_op jit(solution)/shard_map/all_gather | solution.py:77
  458.5 73.3 %psum.46 = f32[16]{0:T(128)S(1)} all-reduce(f32[16]{0:T(128)S(1)} %get-tuple-element.39), channel_id=1, replica_groups=mesh['wide'=32,'narrow'=8] {'wide','narrow'}, use_global_device_ids=true, to_apply=%region_9.0 | all-reduce | flops 16 | bytes 128 | tf_op jit(solution)/shard_map/psum | solution.py:81
  531.9 2.4 collective-permute-start.4
  534.4 3.9 collective-permute-start.5
  539.5 5.6 fusion.61
  546.7 1.3 collective-permute-start.7
  548.0 2.7 collective-permute-start.6
  551.6 1.6 collective-permute-done.6
  553.5 78.3 %psum.47 = f32[16]{0:T(128)S(1)} all-reduce(f32[16]{0:T(128)S(1)} %fusion.15), channel_id=1, replica_groups=mesh['wide'=32,'narrow'=8] {'wide','narrow'}, use_global_device_ids=true, to_apply=%region_11.0 | all-reduce | flops 16 | bytes 128 | tf_op jit(solution)/shard_map/psum | solution.py:118
  (79 shorter events, 22.3 us)
Async XLA Ops:
  7.2 143.6 %copy-start = (f32[1,80,80]{2,1,0:T(8,128)S(1)}, f32[1,80,80]{2,1,0:T(8,128)}, u32[]{:S(2)}) copy-start(f32[1,80,80]{2,1,0:T(8,128)} %param.13) | copy-start | bytes 76804
  7.2 119.2 %all-reduce.6.cloned.1.call-start = ((), (), s32[]{:S(2)}) async-start(), calls=%async_computation | async-start | bytes 327680
  13.7 389.2 %all-reduce.8.cloned.1.call-start = ((), (), s32[]{:S(2)}) async-start(), calls=%async_computation.1 | async-start | bytes 327680
  182.7 17.5 %collective-permute-start.1 = (bf16[16,512]{1,0:T(8,128)(2,1)S(1)}, bf16[16,512]{1,0:T(8,128)(2,1)S(1)}, u32[]{:S(2)}, u32[]{:S(2)}) collective-permute-start(bf16[16,512]{1,0:T(8,128)(2,1)S(1)} %get-tuple-element.30), channel_id=1, source_target_pairs={{0,1},{1,2},{2,3},{3,4},{4,5},{5,6},{6,7},{8,9},{9,10},{10,11},{11... | collective-permute-start | bytes 49160 | tf_op jit(solution)/shard_map/ppermute | solution.py:13
  185.3 16.0 %copy-start.3 = (s32[1,1,4]{2,1,0:T(1,128)S(1)}, s32[1,1,4]{2,1,0:T(1,128)}, u32[]{:S(2)}) copy-start(s32[1,1,4]{2,1,0:T(1,128)} %param.16) | copy-start | bytes 52
  197.6 18.4 %copy-start.1 = (f32[1,1,16,2,512]{4,3,2,1,0:T(2,128)S(1)}, f32[1,1,16,2,512]{4,3,2,1,0:T(2,128)}, u32[]{:S(2)}) copy-start(f32[1,1,16,2,512]{4,3,2,1,0:T(2,128)} %param.9) | copy-start | bytes 196612
  197.6 97.1 %copy-start.2 = (f32[1,1,2,2,8,512]{5,4,3,2,1,0:T(8,128)S(1)}, f32[1,1,2,2,8,512]{5,4,3,2,1,0:T(8,128)}, u32[]{:S(2)}) copy-start(f32[1,1,2,2,8,512]{5,4,3,2,1,0:T(8,128)} %param.12) | copy-start | bytes 196612
  197.6 3.4 collective-permute-start
  208.9 5.4 collective-permute-start.3
  210.2 5.8 collective-permute-start.2
  531.9 6.3 collective-permute-start.4
  534.4 4.5 collective-permute-start.5
  546.7 4.9 collective-permute-start.7
  548.0 5.2 collective-permute-start.6
Sparse Core Ops, SparseCore 0:
  13.8 112.5 all-reduce.5
  296.3 106.6 all-reduce.7
where the time goes:
time: 641 us; the launch traced here: 640 us
  blocking collectives  337 us (53%)
  waiting for transfers between devices  224 us (35%)
  matrix products  21.5 us (3%)
  local copies, waits for them, and re-layouts  18.9 us (3%)
  starting transfers between devices  17.5 us (3%)
  between operations  15 us (2%)
    unnamed x4, waiting for transfers between devices  217 us
    psum x2, blocking collectives, precondition(): lax.psum(jnp.sum(residual * precond, axis=(1, 2)), ('wide', 'narrow'))  152 us
    psum x1, blocking collectives, body(): lax.psum(jnp.sum(direction * applied, axis=(1, 2)), ('wide', 'narrow'))  78.3 us
    all_gather x2, blocking collectives, precondition(): lax.all_gather(solved.reshape(capacity, basis_count * nrhs_count), 'wide'...  60.2 us
    psum x2, blocking collectives, precondition(): lax.psum(owned_rows, 'narrow').reshape(block_order, nrhs_count)  47.1 us
    ppermute x8, starting transfers between devices, shifted(): return lax.ppermute(block, axis, route)  17.5 us
  transfers between devices with their start and end apart: 10, of which 8 were waited for; matrix products, arithmetic and copies ran while one was open for 2% of the time, Pallas kernels for 0%

commit v1 on v0

--- a/solution.py
+++ b/solution.py
@@ -74,8 +74,16 @@
         solved = jnp.dot(
             inverse_block, owner_block, precision=highest, preferred_element_type=jnp.float32
         )
-        all_solved = lax.all_gather(
-            solved.reshape(capacity, basis_count * nrhs_count), "wide", axis=0, tiled=True
+        all_solved = jnp.concatenate(
+            lax.all_to_all(
+                jnp.stack(
+                    [solved.reshape(capacity, basis_count * nrhs_count)] * lax.axis_size("wide")
+                ),
+                "wide",
+                0,
+                0,
+            ),
+            axis=0,
         )
         precond = finish(residual, all_solved)
         inner_value = lax.psum(jnp.sum(residual * precond, axis=(1, 2)), ("wide", "narrow"))

time: 641 us -> 622 us (0.970)
  blocking collectives: 337 us -> 296 us
  starting transfers between devices: 17.5 us -> 28.3 us
  waiting for transfers between devices: 224 us -> 233 us
    all_gather x2 -> x0, blocking collectives: 60.2 us -> none  [precondition(): lax.all_gather(solved.reshape(capacity, basis_count * nrhs_count), 'wide'...]
    all_to_all x0 -> x1, blocking collectives: none -> 19.7 us  [precondition(): lax.all_to_all(jnp.stack([solved.reshape(capacity, basis_count * nrhs_cou...]
    all_to_all x0 -> x1, starting transfers between devices: none -> 10.9 us  [precondition(): lax.all_to_all(jnp.stack([solved.reshape(capacity, basis_count * nrhs_cou...]
    all_to_all x0 -> x1, waiting for transfers between devices: none -> 8.18 us  [precondition(): lax.all_to_all(jnp.stack([solved.reshape(capacity, basis_count * nrhs_cou...]
  transfers between devices with their start and end apart: 10 -> 11, of which waited for: 8 -> 9; matrix products, arithmetic and copies ran while one was open for 2% -> 3% of each run, Pallas kernels for 0% -> 0%
where the time goes in v1:
time: 622 us; the launch traced here: 621 us
  blocking collectives  296 us (48%)
  waiting for transfers between devices  233 us (37%)
  starting transfers between devices  28.3 us (5%)
  matrix products  22.4 us (4%)
  local copies, waits for them, and re-layouts  19.8 us (3%)
  between operations  15 us (2%)
    unnamed x4, waiting for transfers between devices  218 us
    psum x2, blocking collectives, precondition(): lax.psum(jnp.sum(residual * precond, axis=(1, 2)), ('wide', 'narrow'))  152 us
    psum x1, blocking collectives, body(): lax.psum(jnp.sum(direction * applied, axis=(1, 2)), ('wide', 'narrow'))  78.1 us
    psum x2, blocking collectives, precondition(): lax.psum(owned_rows, 'narrow').reshape(block_order, nrhs_count)  47.1 us
    all_to_all x1, blocking collectives, precondition(): lax.all_to_all(jnp.stack([solved.reshape(capacity, basis_count * nrhs_cou...  19.7 us
    ppermute x8, starting transfers between devices, shifted(): return lax.ppermute(block, axis, route)  17.3 us
  transfers between devices with their start and end apart: 11, of which 9 were waited for; matrix products, arithmetic and copies ran while one was open for 3% of the time, Pallas kernels for 0%

profile of v1, /device:TPU:1, one launch (start us, length us, event | category | flops | bytes accessed | tf_op | source)
XLA Modules:
  0.0 620.8 jit_solution(16055537913704447579)
XLA Ops:
  10.6 2.1 pad_add_fusion
  15.7 110.7 %all-reduce.6.cloned.1.call-done = f32[320,128]{1,0:T(8,128)} async-done(((f32[320,128]{1,0:T(8,128)}), f32[320,128]{1,0:T(8,128)}) %all-reduce.6.cloned.1.call-update) | async-done | bytes 163856
  127.2 23.5 %psum.42 = f32[80,16]{1,0:T(8,128)S(1)} all-reduce(f32[80,16]{1,0:T(8,128)S(1)} %reshape.208), channel_id=1, replica_groups=mesh['wide'=32,'narrow'=8] {'narrow'}, use_global_device_ids=true, to_apply=%region_1.0 | all-reduce | flops 1280 | bytes 10240 | tf_op jit(solution)/shard_map/psum | solution.py:73
  151.9 10.9 %all-to-all-start = ((f32[32,10,128]{2,1,0:T(8,128)}), f32[32,10,128]{2,1,0:T(8,128)S(1)}, u32[]{:S(2)}, u32[]{:S(2)}) async-start(f32[32,10,128]{2,1,0:T(8,128)} %stack.62), calls=%async_computation | async-start | bytes 524288 | tf_op jit(solution)/shard_map/all_to_all | solution.py:78
  163.6 8.2 %all-to-all-done = f32[32,10,128]{2,1,0:T(8,128)S(1)} async-done(((f32[32,10,128]{2,1,0:T(8,128)}), f32[32,10,128]{2,1,0:T(8,128)S(1)}, u32[]{:S(2)}, u32[]{:S(2)}) %all-to-all-start) | async-done | bytes 163872 | tf_op jit(solution)/shard_map/all_to_all | solution.py:78
  173.7 1.3 collective-permute-start.1
  176.2 12.3 %copy.64 = bf16[2048,2048]{1,0:T(8,128)(2,1)} copy(bf16[2048,2048]{0,1:T(8,128)(2,1)} %bitcast.220) | data formatting | bytes 16777216 | tf_op jit(solution)/shard_map/dot_general | solution.py:114
  188.5 2.3 collective-permute-start
  192.4 5.6 fusion.64
  199.6 1.3 collective-permute-start.3
  200.9 2.1 collective-permute-start.2
  202.9 1.4 collective-permute-done.3
  204.4 2.3 collective-permute-done.2
  206.8 78.8 %all-reduce.2 = (f32[16]{0:T(128)S(1)}, f32[16]{0:T(128)S(1)}) all-reduce(f32[16]{0:T(128)S(1)} %get-tuple-element.9, f32[16]{0:T(128)S(1)} %get-tuple-element.8), channel_id=1, replica_groups=mesh['wide'=32,'narrow'=8] {'wide','narrow'}, use_global_device_ids=true, to_apply=%region_3.0 | all-reduce | flops 32 | bytes 256 | tf_op jit(solution)/shard_map/psum | solution.py:89
  287.0 106.9 %all-reduce.8.cloned.1.call-done = f32[320,128]{1,0:T(8,128)} async-done(((f32[320,128]{1,0:T(8,128)}), f32[320,128]{1,0:T(8,128)}) %all-reduce.8.cloned.1.call-update) | async-done | bytes 163856
  394.8 23.5 %psum.45 = f32[80,16]{1,0:T(8,128)S(1)} all-reduce(f32[80,16]{1,0:T(8,128)S(1)} %reshape.212), channel_id=1, replica_groups=mesh['wide'=32,'narrow'=8] {'narrow'}, use_global_device_ids=true, to_apply=%region_7.0 | all-reduce | flops 1280 | bytes 10240 | tf_op jit(solution)/shard_map/psum | solution.py:73
  418.7 19.7 %all_to_all.10 = f32[32,10,128]{2,1,0:T(8,128)S(1)} all-to-all(f32[32,10,128]{2,1,0:T(8,128)S(1)} %stack.69), channel_id=1, replica_groups=mesh['wide'=32,'narrow'=8] {'wide'}, dimensions={0} | all-to-all | bytes 327680 | tf_op jit(solution)/shard_map/all_to_all | solution.py:78
  439.6 72.9 %psum.46 = f32[16]{0:T(128)S(1)} all-reduce(f32[16]{0:T(128)S(1)} %get-tuple-element.39), channel_id=1, replica_groups=mesh['wide'=32,'narrow'=8] {'wide','narrow'}, use_global_device_ids=true, to_apply=%region_9.0 | all-reduce | flops 16 | bytes 128 | tf_op jit(solution)/shard_map/psum | solution.py:89
  512.6 2.6 collective-permute-start.4
  515.2 3.9 collective-permute-start.5
  520.4 5.6 fusion.65
  528.9 2.6 collective-permute-start.6
  532.5 1.6 collective-permute-done.6
  534.3 78.1 %psum.47 = f32[16]{0:T(128)S(1)} all-reduce(f32[16]{0:T(128)S(1)} %fusion.15), channel_id=1, replica_groups=mesh['wide'=32,'narrow'=8] {'wide','narrow'}, use_global_device_ids=true, to_apply=%region_11.0 | all-reduce | flops 16 | bytes 128 | tf_op jit(solution)/shard_map/psum | solution.py:126
  (83 shorter events, 25.6 us)
Async XLA Ops:
  7.2 143.6 %copy-start = (f32[1,80,80]{2,1,0:T(8,128)S(1)}, f32[1,80,80]{2,1,0:T(8,128)}, u32[]{:S(2)}) copy-start(f32[1,80,80]{2,1,0:T(8,128)} %param.13) | copy-start | bytes 76804
  7.2 119.2 %all-reduce.6.cloned.1.call-start = ((), (), s32[]{:S(2)}) async-start(), calls=%async_computation.2 | async-start | bytes 327680
  151.9 19.9 %all-to-all-start = ((f32[32,10,128]{2,1,0:T(8,128)}), f32[32,10,128]{2,1,0:T(8,128)S(1)}, u32[]{:S(2)}, u32[]{:S(2)}) async-start(f32[32,10,128]{2,1,0:T(8,128)} %stack.62), calls=%async_computation | async-start | bytes 524288 | tf_op jit(solution)/shard_map/all_to_all | solution.py:78
  162.8 231.2 %all-reduce.8.cloned.1.call-start = ((), (), s32[]{:S(2)}) async-start(), calls=%async_computation.3 | async-start | bytes 327680
  173.7 17.2 %collective-permute-start.1 = (bf16[16,512]{1,0:T(8,128)(2,1)S(1)}, bf16[16,512]{1,0:T(8,128)(2,1)S(1)}, u32[]{:S(2)}, u32[]{:S(2)}) collective-permute-start(bf16[16,512]{1,0:T(8,128)(2,1)S(1)} %get-tuple-element.30), channel_id=1, source_target_pairs={{0,1},{1,2},{2,3},{3,4},{4,5},{5,6},{6,7},{8,9},{9,10},{10,11},{11... | collective-permute-start | bytes 49160 | tf_op jit(solution)/shard_map/ppermute | solution.py:13
  176.2 15.7 %copy-start.3 = (s32[1,1,4]{2,1,0:T(1,128)S(1)}, s32[1,1,4]{2,1,0:T(1,128)}, u32[]{:S(2)}) copy-start(s32[1,1,4]{2,1,0:T(1,128)} %param.16) | copy-start | bytes 52
  188.5 18.1 %copy-start.1 = (f32[1,1,16,2,512]{4,3,2,1,0:T(2,128)S(1)}, f32[1,1,16,2,512]{4,3,2,1,0:T(2,128)}, u32[]{:S(2)}) copy-start(f32[1,1,16,2,512]{4,3,2,1,0:T(2,128)} %param.9) | copy-start | bytes 196612
  188.5 97.0 %copy-start.2 = (f32[1,1,2,2,8,512]{5,4,3,2,1,0:T(8,128)S(1)}, f32[1,1,2,2,8,512]{5,4,3,2,1,0:T(8,128)}, u32[]{:S(2)}) copy-start(f32[1,1,2,2,8,512]{5,4,3,2,1,0:T(8,128)} %param.12) | copy-start | bytes 196612
  188.5 3.2 collective-permute-start
  199.6 4.8 collective-permute-start.3
  200.9 5.7 collective-permute-start.2
  512.6 6.5 %collective-permute-start.4 = (bf16[16,512]{1,0:T(8,128)(2,1)S(1)}, bf16[16,512]{1,0:T(8,128)(2,1)S(1)}, u32[]{:S(2)}, u32[]{:S(2)}) collective-permute-start(bf16[16,512]{1,0:T(8,128)(2,1)S(1)} %get-tuple-element.25), channel_id=1, source_target_pairs={{0,8},{8,16},{16,24},{24,32},{32,40},{40,48},{48,56},{56,64},{64,7... | collective-permute-start | bytes 49160 | tf_op jit(solution)/shard_map/ppermute | solution.py:13
  515.2 4.5 collective-permute-start.5
  527.6 4.9 collective-permute-start.7
  528.9 5.2 collective-permute-start.6
Sparse Core Ops, SparseCore 0:
  13.8 112.5 all-reduce.5
  287.2 106.7 all-reduce.7
